TPU v7x, 256 devices: a whole 4x4x8 slice. The times are simulated.
256 devices in a mesh: depth: 32 (over z, x_hi, core), shot: 8 (over y, x_lo).
Axes of the slice: x: 4 (x_hi: 2, x_lo: 2; x = x_hi * 2 + x_lo), y: 4, z: 8, core: 2. Of those that a mesh axis runs over, the one named last changes fastest.
Arguments:
- courant: float32 [512, 64, 128], P('depth'), may hold values from 0.04 to 0.2
- wave_before: float32 [8, 512, 64, 128], P('shot', 'depth'), may hold values from -10 to 10
- wave_current: float32 [8, 512, 64, 128], P('shot', 'depth'), may hold values from -10 to 10
- adjoint_after: float32 [8, 512, 64, 128], P('shot', 'depth'), may hold values from -10 to 10
- adjoint_current: float32 [8, 512, 64, 128], P('shot', 'depth'), may hold values from -10 to 10
- source_cell: int32 [8], P('shot'), may hold values from 0 to 4194303
- wavelet: float32 [8, 4], P('shot'), may hold values from -15 to 15
- receiver_cell: int32 [8, 256], P('shot'), may hold values from 0 to 4194303
- residual: float32 [8, 4, 256], P('shot'), may hold values from -12 to 12
- history: float32 [2, 5, 512, 64, 128], P(None, None, 'depth', 'shot'), may hold values from -23 to 23, as said below
Outputs:
- gradient: float32 [512, 64, 128], P('depth', 'shot')
- direction: float32 [512, 64, 128], P('depth', 'shot')
- courant_next: float32 [512, 64, 128], P('depth')
Inputs may be any that keep to these rules, and one draw needn't show every extreme that they name: In every pair the sum over all cells of history[0] times history[1] is positive.
All inputs are finite; a program needn't handle non-finite values.
Results may differ from a plain program's by a relative error of at most 0.00026.
Values sent between devices are 32-bit elements; how exact they have to be, the bound alone decides.
A program may use at most 128 MiB of HBM per device.

v0:
```python
import jax
import jax.numpy as jnp
from jax import lax
from jax.sharding import PartitionSpec as P

STEPS = 4
PAIRS = 5
coefficients = (-205.0 / 72.0, 8.0 / 5.0, -1.0 / 5.0, 8.0 / 315.0, -1.0 / 560.0)


def with_halo(cells, sides, width):
    for axis, dim in sides:
        count = lax.axis_size(axis)
        ends = count - 1
        head = lax.slice_in_dim(cells, 0, width, axis=dim)
        tail = lax.slice_in_dim(cells, cells.shape[dim] - width, cells.shape[dim], axis=dim)
        cells = jnp.concatenate(
            [
                lax.ppermute(tail, axis, [(i, (i + 1) % count) for i in range(ends)]),
                cells,
                lax.ppermute(head, axis, [((i + 1) % count, i) for i in range(ends)]),
            ],
            axis=dim,
        )
    return cells


def laplace_core(extended):
    interior = extended[4:-4]
    count_rows = interior.shape[0]
    width_x = interior.shape[1]
    width_y = interior.shape[2]
    padded = jnp.pad(interior, ((0, 0), (4, 4), (4, 4)))
    summed = 3.0 * coefficients[0] * interior
    for reach in range(1, 5):
        weight = coefficients[reach]
        summed = summed + weight * (
            extended[4 + reach : 4 + reach + count_rows]
            + extended[4 - reach : 4 - reach + count_rows]
        )
        summed = summed + weight * (
            padded[:, 4 + reach : 4 + reach + width_x, 4 : 4 + width_y]
            + padded[:, 4 - reach : 4 - reach + width_x, 4 : 4 + width_y]
        )
        summed = summed + weight * (
            padded[:, 4 : 4 + width_x, 4 + reach : 4 + reach + width_y]
            + padded[:, 4 : 4 + width_x, 4 - reach : 4 - reach + width_y]
        )
    return summed


def inject(volume, cell_ids, values, offset):
    count_rows = volume.shape[0]
    plane_size = volume.shape[1] * volume.shape[2]
    depth_row = cell_ids // plane_size - offset
    remainder = cell_ids % plane_size
    inside = (depth_row >= 0) & (depth_row < count_rows)
    row_safe = jnp.clip(depth_row, 0, count_rows - 1)
    return volume.at[row_safe, remainder // volume.shape[2], remainder % volume.shape[2]].add(
        jnp.where(inside, values, jnp.zeros_like(values))
    )


def per_device(
    courant,
    wave_before,
    wave_current,
    adjoint_after,
    adjoint_current,
    source_cell,
    wavelet,
    receiver_cell,
    residual,
    history,
):
    slab_rows = courant.shape[0]
    first_row = lax.axis_index("depth") * slab_rows
    shot_count = lax.axis_size("shot")
    summed = jnp.zeros(courant.shape, jnp.float32)
    laplacians = []
    wave_old = wave_before[0]
    wave_now = wave_current[0]
    for moment in range(STEPS):
        extended = with_halo(wave_now, (("depth", 0),), 4)
        laplacian = laplace_core(extended)
        wave_new = 2.0 * wave_now - wave_old + courant * laplacian
        wave_new = inject(wave_new, source_cell, wavelet[0, moment : moment + 1], first_row)
        laplacians.append(laplacian)
        wave_old, wave_now = (wave_now, wave_new)
    adjoint_old = adjoint_after[0]
    adjoint_now = adjoint_current[0]
    for moment in reversed(range(STEPS)):
        extended = with_halo(courant * adjoint_now, (("depth", 0),), 4)
        adjoint_new = 2.0 * adjoint_now - adjoint_old + laplace_core(extended)
        adjoint_new = inject(adjoint_new, receiver_cell[0], residual[0, moment], first_row)
        summed = summed + adjoint_new * laplacians[moment]
        adjoint_old, adjoint_now = (adjoint_now, adjoint_new)
    grad_piece = lax.psum_scatter(summed, "shot", scatter_dimension=1, tiled=True) * (
        1.0 / (shot_count * STEPS)
    )
    displaced = history[0]
    changes = history[1]
    step_change = jnp.einsum("izxy,jzxy->ij", displaced, changes, precision=lax.Precision.HIGHEST)
    change_change = jnp.einsum("izxy,jzxy->ij", changes, changes, precision=lax.Precision.HIGHEST)
    step_grad = jnp.sum(displaced * grad_piece, axis=(1, 2, 3))
    change_grad = jnp.sum(changes * grad_piece, axis=(1, 2, 3))
    packed = jnp.concatenate(
        [step_change, change_change, step_grad[None], change_grad[None]], axis=0
    )
    packed = lax.psum(packed, ("depth", "shot"))
    step_change = packed[:PAIRS]
    change_change = packed[PAIRS : 2 * PAIRS]
    step_grad = packed[2 * PAIRS]
    change_grad = packed[2 * PAIRS + 1]
    inverse = [1.0 / step_change[i, i] for i in range(PAIRS)]
    alphas = [None] * PAIRS
    for i in reversed(range(PAIRS)):
        value = step_grad[i]
        for j in range(i + 1, PAIRS):
            value = value - alphas[j] * step_change[i, j]
        alphas[i] = inverse[i] * value
    gamma = step_change[PAIRS - 1, PAIRS - 1] / change_change[PAIRS - 1, PAIRS - 1]
    gains = []
    for i in range(PAIRS):
        value = change_grad[i]
        for j in range(PAIRS):
            value = value - alphas[j] * change_change[i, j]
        value = gamma * value
        for j in range(i):
            value = value + gains[j] * step_change[j, i]
        gains.append(alphas[i] - inverse[i] * value)
    scaled = grad_piece
    for i in range(PAIRS):
        scaled = scaled - alphas[i] * changes[i]
    scaled = gamma * scaled
    for i in range(PAIRS):
        scaled = scaled + gains[i] * displaced[i]
    direction = -scaled
    piece_width = grad_piece.shape[1]
    own_courant = lax.dynamic_slice_in_dim(
        courant, lax.axis_index("shot") * piece_width, piece_width, 1
    )
    next_piece = own_courant + 0.05 * direction
    courant_next = lax.all_gather(next_piece, "shot", axis=1, tiled=True)
    return (grad_piece, direction, courant_next)


def solution(mesh):
    return jax.shard_map(
        per_device,
        mesh=mesh,
        in_specs=(
            P("depth", None, None),
            P("shot", "depth", None, None),
            P("shot", "depth", None, None),
            P("shot", "depth", None, None),
            P("shot", "depth", None, None),
            P("shot"),
            P("shot", None),
            P("shot", None),
            P("shot", None, None),
            P(None, None, "depth", "shot", None),
        ),
        out_specs=(P("depth", "shot", None), P("depth", "shot", None), P("depth", None, None)),
        check_vma=False,
    )
```

profile of v0, /device:TPU:32, one launch (start us, length us, event | category | flops | bytes accessed | tf_op | source)
XLA Modules:
  0.0 397.9 jit_solution(11437620847095359479)
XLA Ops:
  7.2 1.3 bitcast_multiply_fusion
  8.6 4.0 %collective-permute-start = (f32[4,64,128]{2,1,0:T(8,128)S(1)}, f32[4,64,128]{2,1,0:T(8,128)S(1)}, u32[]{:S(2)}, u32[]{:S(2)}) collective-permute-start(f32[4,64,128]{2,1,0:T(8,128)S(1)} %get-tuple-element.70), channel_id=1, source_target_pairs={{8,0},{16,8},{24,16},{32,24},{40,32},{48,40},{56,48},{64,56},{72,6... | collective-permute-start | bytes 393224 | tf_op jit(solution)/shard_map/ppermute | solution.py:21
  12.7 1.9 collective-permute-start.1
  14.7 6.0 %collective-permute-start.2 = (f32[4,64,128]{2,1,0:T(8,128)S(1)}, f32[4,64,128]{2,1,0:T(8,128)S(1)}, u32[]{:S(2)}, u32[]{:S(2)}) collective-permute-start(f32[4,64,128]{2,1,0:T(8,128)S(1)} %get-tuple-element.68), channel_id=1, source_target_pairs={{8,0},{16,8},{24,16},{32,24},{40,32},{48,40},{56,48},{64,56},{72,6... | collective-permute-start | bytes 393224 | tf_op jit(solution)/shard_map/ppermute | solution.py:21
  20.7 1.9 collective-permute-start.3
  23.3 0.7 fusion.369
  26.7 0.7 and_reduce_fusion
  27.4 1.9 fusion.184
  29.4 23.9 %scatter_fusion = f32[16,64,128]{2,1,0:T(8,128)S(1)} fusion(f32[16,64,128]{2,1,0:T(8,128)S(1)} %fusion.184, s32[256]{0:T(256)S(1)} %bitcast.180, f32[256]{0:T(256)} %get-tuple-element.128), kind=kCustom, calls=%fused_computation | custom fusion | flops 256 | bytes 6144 | tf_op jit(solution)/shard_map/scatter-add | solution.py:59
  53.4 3.7 fusion.348
  57.0 0.7 dynamic-slice.24
  59.8 6.1 %collective-permute-start.10 = (f32[4,64,128]{2,1,0:T(8,128)S(1)}, f32[4,64,128]{2,1,0:T(8,128)S(1)}, u32[]{:S(2)}, u32[]{:S(2)}) collective-permute-start(f32[4,64,128]{2,1,0:T(8,128)S(1)} %get-tuple-element.59), channel_id=1, source_target_pairs={{8,0},{16,8},{24,16},{32,24},{40,32},{48,40},{56,48},{64,56},{72,6... | collective-permute-start | bytes 393224 | tf_op jit(solution)/shard_map/ppermute | solution.py:21
  65.9 1.9 collective-permute-start.11
  67.8 0.7 fusion.363
  68.5 6.0 %collective-permute-start.4 = (f32[4,64,128]{2,1,0:T(8,128)}, f32[4,64,128]{2,1,0:T(8,128)S(1)}, u32[]{:S(2)}, u32[]{:S(2)}) collective-permute-start(f32[4,64,128]{2,1,0:T(8,128)} %get-tuple-element.66), channel_id=1, source_target_pairs={{8,0},{16,8},{24,16},{32,24},{40,32},{48,40},{56,48},{64,56},{72,6... | collective-permute-start | bytes 393224 | tf_op jit(solution)/shard_map/ppermute | solution.py:21
  74.5 1.9 collective-permute-start.5
  76.5 9.1 %fusion.59 = f32[16,64,128]{2,1,0:T(8,128)S(1)} fusion(f32[16,64,128]{2,1,0:T(8,128)} %copy-done.6, f32[4,64,128]{2,1,0:T(8,128)S(1)} %collective-permute-done.11, f32[4,64,128]{2,1,0:T(8,128)S(1)} %collective-permute-done.10, f32[1,16,64,128]{3,2,1,0:T(8,128)S(1)} %copy-done.2, f32[16,64,128]{2,1,0:T(8,128)S(1)} %scatter_fusion), kind=kLoop, calls=%fused_computation.289 | loop fusion | flops 6291456 | bytes 2359296 | tf_op jit(solution)/shard_map/add | solution.py:94
  85.6 15.2 %scatter_fusion.1 = f32[16,64,128]{2,1,0:T(8,128)S(1)} fusion(f32[16,64,128]{2,1,0:T(8,128)S(1)} %fusion.59, s32[256]{0:T(256)S(1)} %bitcast.181, f32[256]{0:T(256)S(1)} %get-tuple-element.127), kind=kCustom, calls=%fused_computation.1 | custom fusion | flops 256 | bytes 6144 | tf_op jit(solution)/shard_map/scatter-add | solution.py:59
  100.9 2.7 multiply_add_fusion.1
  103.6 6.1 %collective-permute-start.12 = (f32[4,64,128]{2,1,0:T(8,128)S(1)}, f32[4,64,128]{2,1,0:T(8,128)S(1)}, u32[]{:S(2)}, u32[]{:S(2)}) collective-permute-start(f32[4,64,128]{2,1,0:T(8,128)S(1)} %get-tuple-element.56), channel_id=1, source_target_pairs={{8,0},{16,8},{24,16},{32,24},{40,32},{48,40},{56,48},{64,56},{72,6... | collective-permute-start | bytes 393224 | tf_op jit(solution)/shard_map/ppermute | solution.py:21
  109.7 1.9 collective-permute-start.13
  111.6 0.6 dynamic-slice.25
  114.3 0.7 fusion.362
  115.0 6.0 %collective-permute-start.6 = (f32[4,64,128]{2,1,0:T(8,128)}, f32[4,64,128]{2,1,0:T(8,128)S(1)}, u32[]{:S(2)}, u32[]{:S(2)}) collective-permute-start(f32[4,64,128]{2,1,0:T(8,128)} %get-tuple-element.64), channel_id=1, source_target_pairs={{8,0},{16,8},{24,16},{32,24},{40,32},{48,40},{56,48},{64,56},{72,6... | collective-permute-start | bytes 393224 | tf_op jit(solution)/shard_map/ppermute | solution.py:21
  121.1 1.9 collective-permute-start.7
  123.0 2.0 fusion.34
  125.0 15.2 %scatter_fusion.2 = f32[16,64,128]{2,1,0:T(8,128)S(1)} fusion(f32[16,64,128]{2,1,0:T(8,128)S(1)} %fusion.34, s32[256]{0:T(256)S(1)} %bitcast.182, f32[256]{0:T(256)S(1)} %get-tuple-element.126), kind=kCustom, calls=%fused_computation.2 | custom fusion | flops 256 | bytes 6144 | tf_op jit(solution)/shard_map/scatter-add | solution.py:59
  140.2 10.6 %multiply_add_fusion = (f32[16,64,128]{2,1,0:T(8,128)S(1)}, f32[16,64,128]{2,1,0:T(8,128)}, f32[16,64,128]{2,1,0:T(8,128)S(1)}) fusion(f32[16,64,128]{2,1,0:T(8,128)S(1)} %copy-done, f32[16,64,128]{2,1,0:T(8,128)S(1)} %scatter-add.44, f32[16,64,128]{2,1,0:T(8,128)} %copy-done.3, f32[4,64,128]{2,1,0:T(8,128)} %collective-permute-done.7, ...), kind=kLoop, calls=%fused_computation.602 | loop fusion | flops 6553600 | bytes 3932160 | tf_op jit(solution)/shard_map/add | solution.py:86
  150.9 6.1 %collective-permute-start.14 = (f32[4,64,128]{2,1,0:T(8,128)S(1)}, f32[4,64,128]{2,1,0:T(8,128)S(1)}, u32[]{:S(2)}, u32[]{:S(2)}) collective-permute-start(f32[4,64,128]{2,1,0:T(8,128)S(1)} %get-tuple-element.53), channel_id=1, source_target_pairs={{8,0},{16,8},{24,16},{32,24},{40,32},{48,40},{56,48},{64,56},{72,6... | collective-permute-start | bytes 393224 | tf_op jit(solution)/shard_map/ppermute | solution.py:21
  156.9 2.1 collective-permute-start.15
  161.7 0.7 fusion.361
  162.4 6.0 %collective-permute-start.8 = (f32[4,64,128]{2,1,0:T(8,128)}, f32[4,64,128]{2,1,0:T(8,128)S(1)}, u32[]{:S(2)}, u32[]{:S(2)}) collective-permute-start(f32[4,64,128]{2,1,0:T(8,128)} %get-tuple-element.62), channel_id=1, source_target_pairs={{8,0},{16,8},{24,16},{32,24},{40,32},{48,40},{56,48},{64,56},{72,6... | collective-permute-start | bytes 393224 | tf_op jit(solution)/shard_map/ppermute | solution.py:21
  168.5 1.9 collective-permute-start.9
  170.4 2.2 fusion.9
  172.7 15.2 %scatter_fusion.3 = f32[16,64,128]{2,1,0:T(8,128)S(1)} fusion(f32[16,64,128]{2,1,0:T(8,128)S(1)} %fusion.9, s32[256]{0:T(256)S(1)} %bitcast.183, f32[256]{0:T(256)S(1)} %get-tuple-element.43), kind=kCustom, calls=%fused_computation.3 | custom fusion | flops 256 | bytes 6144 | tf_op jit(solution)/shard_map/scatter-add | solution.py:59
  187.9 3.9 fusion.87
  191.9 1.1 fusion.357
  193.0 1.2 convolution_bitcast_fusion
  194.2 1.4 convolution_bitcast_fusion.1
  195.6 48.2 %reduce-scatter.2.cloned.1.call-done = f32[16,8,128]{2,1,0:T(8,128)} async-done(((f32[16,64,128]{2,1,0:T(8,128)}), f32[16,8,128]{2,1,0:T(8,128)}) %reduce-scatter.2.cloned.1.call-update) | async-done | bytes 65552 | tf_op jit(solution)/shard_map/reduce_scatter | solution.py:98
  243.7 0.8 broadcast_multiply_fusion
  245.4 73.3 %psum.7 = f32[12,5]{0,1:T(8,128)S(1)} all-reduce(f32[12,5]{0,1:T(8,128)S(1)} %pad_maximum_fusion.16), channel_id=1, replica_groups=mesh['depth'=32,'shot'=8] {'depth','shot'}, use_global_device_ids=true, to_apply=%region_8.9 | all-reduce | flops 60 | bytes 480 | tf_op jit(solution)/shard_map/psum | solution.py:110
  318.8 0.7 fusion.366
  319.5 0.7 fusion.367
  320.2 0.7 fusion.365
  359.7 0.7 multiply_add_fusion.2
  360.4 29.8 %all_gather.3 = f32[16,64,128]{2,1,0:T(8,128)S(1)} all-gather(f32[16,8,128]{2,1,0:T(8,128)S(1)} %get-tuple-element.41), channel_id=1, replica_groups=mesh['depth'=32,'shot'=8] {'shot'}, dimensions={1}, use_global_device_ids=true | all-gather | bytes 589824 | tf_op jit(solution)/shard_map/all_gather | solution.py:144
  390.3 0.8 copy.49
  (70 shorter events, 2.7 us)
Async XLA Ops:
  7.2 236.6 %reduce-scatter.2.cloned.1.call-start = ((), (), s32[]{:S(2)}) async-start(), calls=%async_computation.1 | async-start | bytes 589824 | tf_op jit(solution)/shard_map/reduce_scatter | solution.py:98
  7.2 20.2 %copy-start.10 = (f32[1,16,64,128]{3,2,1,0:T(8,128)S(1)}, f32[1,16,64,128]{3,2,1,0:T(8,128)}, u32[]{:S(2)}) copy-start(f32[1,16,64,128]{3,2,1,0:T(8,128)} %param.19) | copy-start | bytes 1572868
  8.5 6.1 %copy-start.1 = (f32[1,16,64,128]{3,2,1,0:T(8,128)S(1)}, f32[1,16,64,128]{3,2,1,0:T(8,128)}, u32[]{:S(2)}) copy-start(f32[1,16,64,128]{3,2,1,0:T(8,128)} %param.18) | copy-start | bytes 1572868
  8.6 14.1 %copy-start.14 = (f32[1,4,256]{2,1,0:T(4,128)S(1)}, f32[1,4,256]{2,1,0:T(4,128)}, u32[]{:S(2)}) copy-start(f32[1,4,256]{2,1,0:T(4,128)} %param.24) | copy-start | bytes 12292
  8.6 14.1 %copy-start.15 = (s32[1,256]{1,0:T(1,128)S(1)}, s32[1,256]{1,0:T(1,128)}, u32[]{:S(2)}) copy-start(s32[1,256]{1,0:T(1,128)} %param.23) | copy-start | bytes 3076
  8.6 14.7 %copy-start.13 = (f32[1,4]{1,0:T(1,128)S(1)}, f32[1,4]{1,0:T(1,128)}, u32[]{:S(2)}) copy-start(f32[1,4]{1,0:T(1,128)} %param.22) | copy-start | bytes 52
  8.6 18.1 %copy-start.16 = (s32[3]{0:T(128)S(1)}, s32[3]{0:T(128)}, u32[]{:S(2)}) copy-start(s32[3]{0:T(128)} %constant.255.clone.1) | copy-start | bytes 40
  8.6 18.8 %copy-start.2 = (f32[1,16,64,128]{3,2,1,0:T(8,128)S(1)}, f32[1,16,64,128]{3,2,1,0:T(8,128)}, u32[]{:S(2)}) copy-start(f32[1,16,64,128]{3,2,1,0:T(8,128)} %param.20) | copy-start | bytes 1572868
  8.6 18.8 %collective-permute-start = (f32[4,64,128]{2,1,0:T(8,128)S(1)}, f32[4,64,128]{2,1,0:T(8,128)S(1)}, u32[]{:S(2)}, u32[]{:S(2)}) collective-permute-start(f32[4,64,128]{2,1,0:T(8,128)S(1)} %get-tuple-element.70), channel_id=1, source_target_pairs={{8,0},{16,8},{24,16},{32,24},{40,32},{48,40},{56,48},{64,56},{72,6... | collective-permute-start | bytes 393224 | tf_op jit(solution)/shard_map/ppermute | solution.py:21
  12.7 14.7 %collective-permute-start.1 = (f32[4,64,128]{2,1,0:T(8,128)S(1)}, f32[4,64,128]{2,1,0:T(8,128)S(1)}, u32[]{:S(2)}, u32[]{:S(2)}) collective-permute-start(f32[4,64,128]{2,1,0:T(8,128)S(1)} %get-tuple-element.71), channel_id=1, source_target_pairs={{0,8},{8,16},{16,24},{24,32},{32,40},{40,48},{48,56},{56,64},{64,7... | collective-permute-start | bytes 393224 | tf_op jit(solution)/shard_map/ppermute | solution.py:19
  14.7 38.7 %collective-permute-start.2 = (f32[4,64,128]{2,1,0:T(8,128)S(1)}, f32[4,64,128]{2,1,0:T(8,128)S(1)}, u32[]{:S(2)}, u32[]{:S(2)}) collective-permute-start(f32[4,64,128]{2,1,0:T(8,128)S(1)} %get-tuple-element.68), channel_id=1, source_target_pairs={{8,0},{16,8},{24,16},{32,24},{40,32},{48,40},{56,48},{64,56},{72,6... | collective-permute-start | bytes 393224 | tf_op jit(solution)/shard_map/ppermute | solution.py:21
  20.7 32.6 %collective-permute-start.3 = (f32[4,64,128]{2,1,0:T(8,128)S(1)}, f32[4,64,128]{2,1,0:T(8,128)S(1)}, u32[]{:S(2)}, u32[]{:S(2)}) collective-permute-start(f32[4,64,128]{2,1,0:T(8,128)S(1)} %get-tuple-element.69), channel_id=1, source_target_pairs={{0,8},{8,16},{16,24},{24,32},{32,40},{40,48},{48,56},{56,64},{64,7... | collective-permute-start | bytes 393224 | tf_op jit(solution)/shard_map/ppermute | solution.py:19
  29.4 24.0 %copy-start = (f32[16,64,128]{2,1,0:T(8,128)S(1)}, f32[16,64,128]{2,1,0:T(8,128)}, u32[]{:S(2)}) copy-start(f32[16,64,128]{2,1,0:T(8,128)} %param.16) | copy-start | bytes 1572868
  57.0 19.4 %copy-start.6 = (f32[16,64,128]{2,1,0:T(8,128)}, f32[16,64,128]{2,1,0:T(8,128)S(1)}, u32[]{:S(2)}) copy-start(f32[16,64,128]{2,1,0:T(8,128)S(1)} %get-tuple-element.61) | copy-start | bytes 1572868
  59.8 16.6 %collective-permute-start.10 = (f32[4,64,128]{2,1,0:T(8,128)S(1)}, f32[4,64,128]{2,1,0:T(8,128)S(1)}, u32[]{:S(2)}, u32[]{:S(2)}) collective-permute-start(f32[4,64,128]{2,1,0:T(8,128)S(1)} %get-tuple-element.59), channel_id=1, source_target_pairs={{8,0},{16,8},{24,16},{32,24},{40,32},{48,40},{56,48},{64,56},{72,6... | collective-permute-start | bytes 393224 | tf_op jit(solution)/shard_map/ppermute | solution.py:21
  65.9 10.6 %collective-permute-start.11 = (f32[4,64,128]{2,1,0:T(8,128)S(1)}, f32[4,64,128]{2,1,0:T(8,128)S(1)}, u32[]{:S(2)}, u32[]{:S(2)}) collective-permute-start(f32[4,64,128]{2,1,0:T(8,128)S(1)} %get-tuple-element.60), channel_id=1, source_target_pairs={{0,8},{8,16},{16,24},{24,32},{32,40},{40,48},{48,56},{56,64},{64,7... | collective-permute-start | bytes 393224 | tf_op jit(solution)/shard_map/ppermute | solution.py:19
  68.5 32.4 %collective-permute-start.4 = (f32[4,64,128]{2,1,0:T(8,128)}, f32[4,64,128]{2,1,0:T(8,128)S(1)}, u32[]{:S(2)}, u32[]{:S(2)}) collective-permute-start(f32[4,64,128]{2,1,0:T(8,128)} %get-tuple-element.66), channel_id=1, source_target_pairs={{8,0},{16,8},{24,16},{32,24},{40,32},{48,40},{56,48},{64,56},{72,6... | collective-permute-start | bytes 393224 | tf_op jit(solution)/shard_map/ppermute | solution.py:21
  74.5 26.3 %collective-permute-start.5 = (f32[4,64,128]{2,1,0:T(8,128)S(1)}, f32[4,64,128]{2,1,0:T(8,128)S(1)}, u32[]{:S(2)}, u32[]{:S(2)}) collective-permute-start(f32[4,64,128]{2,1,0:T(8,128)S(1)} %get-tuple-element.67), channel_id=1, source_target_pairs={{0,8},{8,16},{16,24},{24,32},{32,40},{40,48},{48,56},{56,64},{64,7... | collective-permute-start | bytes 393224 | tf_op jit(solution)/shard_map/ppermute | solution.py:19
  103.6 9.3 %copy-start.7 = (f32[16,64,128]{2,1,0:T(8,128)}, f32[16,64,128]{2,1,0:T(8,128)S(1)}, u32[]{:S(2)}) copy-start(f32[16,64,128]{2,1,0:T(8,128)S(1)} %get-tuple-element.58) | copy-start | bytes 1572868
  103.6 19.4 %collective-permute-start.12 = (f32[4,64,128]{2,1,0:T(8,128)S(1)}, f32[4,64,128]{2,1,0:T(8,128)S(1)}, u32[]{:S(2)}, u32[]{:S(2)}) collective-permute-start(f32[4,64,128]{2,1,0:T(8,128)S(1)} %get-tuple-element.56), channel_id=1, source_target_pairs={{8,0},{16,8},{24,16},{32,24},{40,32},{48,40},{56,48},{64,56},{72,6... | collective-permute-start | bytes 393224 | tf_op jit(solution)/shard_map/ppermute | solution.py:21
  109.7 13.3 %collective-permute-start.13 = (f32[4,64,128]{2,1,0:T(8,128)S(1)}, f32[4,64,128]{2,1,0:T(8,128)S(1)}, u32[]{:S(2)}, u32[]{:S(2)}) collective-permute-start(f32[4,64,128]{2,1,0:T(8,128)S(1)} %get-tuple-element.57), channel_id=1, source_target_pairs={{0,8},{8,16},{16,24},{24,32},{32,40},{40,48},{48,56},{56,64},{64,7... | collective-permute-start | bytes 393224 | tf_op jit(solution)/shard_map/ppermute | solution.py:19
  114.3 10.7 %copy-start.3 = (f32[16,64,128]{2,1,0:T(8,128)}, f32[16,64,128]{2,1,0:T(8,128)S(1)}, u32[]{:S(2)}) copy-start(f32[16,64,128]{2,1,0:T(8,128)S(1)} %scatter-add.45) | copy-start | bytes 1572868
  114.3 8.7 %copy-start.8 = (f32[16,64,128]{2,1,0:T(8,128)S(1)}, f32[16,64,128]{2,1,0:T(8,128)}, u32[]{:S(2)}) copy-start(f32[16,64,128]{2,1,0:T(8,128)} %copy-done.7) | copy-start | bytes 1572868
  115.0 25.2 %collective-permute-start.6 = (f32[4,64,128]{2,1,0:T(8,128)}, f32[4,64,128]{2,1,0:T(8,128)S(1)}, u32[]{:S(2)}, u32[]{:S(2)}) collective-permute-start(f32[4,64,128]{2,1,0:T(8,128)} %get-tuple-element.64), channel_id=1, source_target_pairs={{8,0},{16,8},{24,16},{32,24},{40,32},{48,40},{56,48},{64,56},{72,6... | collective-permute-start | bytes 393224 | tf_op jit(solution)/shard_map/ppermute | solution.py:21
  121.1 19.2 %collective-permute-start.7 = (f32[4,64,128]{2,1,0:T(8,128)}, f32[4,64,128]{2,1,0:T(8,128)}, u32[]{:S(2)}, u32[]{:S(2)}) collective-permute-start(f32[4,64,128]{2,1,0:T(8,128)} %get-tuple-element.65), channel_id=1, source_target_pairs={{0,8},{8,16},{16,24},{24,32},{32,40},{40,48},{48,56},{56,64},{64,7... | collective-permute-start | bytes 393224 | tf_op jit(solution)/shard_map/ppermute | solution.py:19
  150.8 9.5 %copy-start.4 = (f32[16,64,128]{2,1,0:T(8,128)}, f32[16,64,128]{2,1,0:T(8,128)S(1)}, u32[]{:S(2)}) copy-start(f32[16,64,128]{2,1,0:T(8,128)S(1)} %get-tuple-element.55) | copy-start | bytes 1572868
  150.9 19.6 %collective-permute-start.14 = (f32[4,64,128]{2,1,0:T(8,128)S(1)}, f32[4,64,128]{2,1,0:T(8,128)S(1)}, u32[]{:S(2)}, u32[]{:S(2)}) collective-permute-start(f32[4,64,128]{2,1,0:T(8,128)S(1)} %get-tuple-element.53), channel_id=1, source_target_pairs={{8,0},{16,8},{24,16},{32,24},{40,32},{48,40},{56,48},{64,56},{72,6... | collective-permute-start | bytes 393224 | tf_op jit(solution)/shard_map/ppermute | solution.py:21
  156.9 13.5 %collective-permute-start.15 = (f32[4,64,128]{2,1,0:T(8,128)S(1)}, f32[4,64,128]{2,1,0:T(8,128)}, u32[]{:S(2)}, u32[]{:S(2)}) collective-permute-start(f32[4,64,128]{2,1,0:T(8,128)S(1)} %get-tuple-element.54), channel_id=1, source_target_pairs={{0,8},{8,16},{16,24},{24,32},{32,40},{40,48},{48,56},{56,64},{64,7... | collective-permute-start | bytes 393224 | tf_op jit(solution)/shard_map/ppermute | solution.py:19
  161.7 8.7 %copy-start.5 = (f32[16,64,128]{2,1,0:T(8,128)S(1)}, f32[16,64,128]{2,1,0:T(8,128)}, u32[]{:S(2)}) copy-start(f32[16,64,128]{2,1,0:T(8,128)} %copy-done.4) | copy-start | bytes 1572868
  162.4 25.5 %collective-permute-start.8 = (f32[4,64,128]{2,1,0:T(8,128)}, f32[4,64,128]{2,1,0:T(8,128)S(1)}, u32[]{:S(2)}, u32[]{:S(2)}) collective-permute-start(f32[4,64,128]{2,1,0:T(8,128)} %get-tuple-element.62), channel_id=1, source_target_pairs={{8,0},{16,8},{24,16},{32,24},{40,32},{48,40},{56,48},{64,56},{72,6... | collective-permute-start | bytes 393224 | tf_op jit(solution)/shard_map/ppermute | solution.py:21
  168.5 19.4 %collective-permute-start.9 = (f32[4,64,128]{2,1,0:T(8,128)}, f32[4,64,128]{2,1,0:T(8,128)S(1)}, u32[]{:S(2)}, u32[]{:S(2)}) collective-permute-start(f32[4,64,128]{2,1,0:T(8,128)} %get-tuple-element.63), channel_id=1, source_target_pairs={{0,8},{8,16},{16,24},{24,32},{32,40},{40,48},{48,56},{56,64},{64,7... | collective-permute-start | bytes 393224 | tf_op jit(solution)/shard_map/ppermute | solution.py:19
  244.6 111.4 %copy-start.12 = (f32[16,8,128]{2,1,0:T(8,128)}, f32[16,8,128]{2,1,0:T(8,128)S(1)}, u32[]{:S(2)}) copy-start(f32[16,8,128]{2,1,0:T(8,128)S(1)} %broadcast_multiply_fusion) | copy-start | bytes 196612
  244.6 115.1 %copy-start.9 = (f32[2,5,16,8,128]{4,3,2,1,0:T(8,128)S(1)}, f32[2,5,16,8,128]{4,3,2,1,0:T(8,128)}, u32[]{:S(2)}) copy-start(f32[2,5,16,8,128]{4,3,2,1,0:T(8,128)} %param.25) | copy-start | bytes 1966084
  244.6 115.1 %copy-start.11 = (f32[16,8,128]{2,1,0:T(8,128)S(1)}, f32[16,8,128]{2,1,0:T(8,128)}, u32[]{:S(2)}) copy-start(f32[16,8,128]{2,1,0:T(8,128)} %reduce-scatter.2.cloned.1.call-done) | copy-start | bytes 196612
Sparse Core Ops, SparseCore 0:
  192.0 51.6 reduce-scatter.1
where the time goes:
time: 400 us; the launch traced here: 398 us
  other arithmetic  111 us (28%)
  blocking collectives  103 us (26%)
  starting transfers between devices  61.9 us (15%)
  between operations  61.9 us (15%)
  waiting for transfers between devices  48.2 us (12%)
  local copies, waits for them, and re-layouts  9.48 us (2%)
    psum x1, blocking collectives, per_device(): packed = lax.psum(packed, ('depth', 'shot'))  73.3 us
    scatter-add x4, other arithmetic, inject(): volume.at[row_safe, remainder // volume.shape[2], remainder % volume.shap...  69.6 us
    reduce_scatter x1, waiting for transfers between devices, per_device(): lax.psum_scatter(summed, 'shot', scatter_dimension=1, tiled=True)  48.2 us
    ppermute x8, starting transfers between devices, with_halo(): lax.ppermute(head, axis, [((i + 1) % count, i) for i in range(ends)])  46.4 us
    all_gather x1, blocking collectives, per_device(): courant_next = lax.all_gather(next_piece, 'shot', axis=1, tiled=True)  29.8 us
    add x3, other arithmetic, per_device(): wave_new = 2.0 * wave_now - wave_old + courant * laplacian  17 us
    ppermute x8, starting transfers between devices, with_halo(): lax.ppermute(tail, axis, [(i, (i + 1) % count) for i in range(ends)])  15.5 us
    add x4, other arithmetic, per_device(): adjoint_new = 2.0 * adjoint_now - adjoint_old + laplace_core(extended)  15.3 us
  transfers between devices with their start and end apart: 17, of which 1 were waited for; matrix products, arithmetic and copies ran while one was open for 24% of the time, Pallas kernels for 0%

commit v1 on v0

--- a/solution.py
+++ b/solution.py
@@ -107,7 +107,8 @@
     packed = jnp.concatenate(
         [step_change, change_change, step_grad[None], change_grad[None]], axis=0
     )
-    packed = lax.psum(packed, ("depth", "shot"))
+    parts = lax.all_gather(packed, ("depth", "shot"))
+    packed = jnp.sum(parts, axis=0)
     step_change = packed[:PAIRS]
     change_change = packed[PAIRS : 2 * PAIRS]
     step_grad = packed[2 * PAIRS]

time: 400 us -> 962 us (2.40)
  the two profiles are of different devices: /device:TPU:32 before, /device:TPU:128 now
where the time goes in v1:
time: 962 us; the launch traced here: 960 us
  blocking collectives  655 us (68%)
  other arithmetic  123 us (13%)
  starting transfers between devices  70.2 us (7%)
  between operations  61.7 us (6%)
  waiting for transfers between devices  39 us (4%)
    all_gather x1, blocking collectives, per_device(): parts = lax.all_gather(packed, ('depth', 'shot'))  625 us
    scatter-add x4, other arithmetic, inject(): volume.at[row_safe, remainder // volume.shape[2], remainder % volume.shap...  69.3 us
    ppermute x8, starting transfers between devices, with_halo(): lax.ppermute(head, axis, [((i + 1) % count, i) for i in range(ends)])  54.6 us
    reduce_scatter x1, waiting for transfers between devices, per_device(): lax.psum_scatter(summed, 'shot', scatter_dimension=1, tiled=True)  38.9 us
    all_gather x1, blocking collectives, per_device(): courant_next = lax.all_gather(next_piece, 'shot', axis=1, tiled=True)  29.8 us
    add x4, other arithmetic, per_device(): adjoint_new = 2.0 * adjoint_now - adjoint_old + laplace_core(extended)  28.2 us
  transfers between devices with their start and end apart: 17, of which 1 were waited for; matrix products, arithmetic and copies ran while one was open for 11% of the time, Pallas kernels for 0%

profile of v1, /device:TPU:128, one launch (start us, length us, event | category | flops | bytes accessed | tf_op | source)
XLA Modules:
  0.0 960.5 jit_solution(6491742489121263552)
XLA Ops:
  7.3 1.4 bitcast_multiply_fusion
  8.7 3.9 collective-permute-start
  12.6 1.9 collective-permute-start.1
  14.6 7.3 collective-permute-start.2
  21.8 1.9 collective-permute-start.3
  27.7 0.8 and_reduce_fusion
  28.4 1.9 fusion.184
  30.4 23.9 %scatter_fusion = f32[16,64,128]{2,1,0:T(8,128)S(1)} fusion(f32[16,64,128]{2,1,0:T(8,128)S(1)} %fusion.184, s32[256]{0:T(256)S(1)} %bitcast.182, f32[256]{0:T(256)} %get-tuple-element.128), kind=kCustom, calls=%fused_computation | custom fusion | flops 256 | bytes 6144 | tf_op jit(solution)/shard_map/scatter-add | solution.py:59
  54.3 3.7 fusion.348
  58.0 0.7 dynamic-slice.24
  60.7 7.2 collective-permute-start.10
  68.0 1.9 collective-permute-start.11
  69.9 0.7 fusion.363
  70.6 7.2 collective-permute-start.4
  77.9 1.9 collective-permute-start.5
  79.8 9.0 fusion.59
  88.9 15.1 %scatter_fusion.1 = f32[16,64,128]{2,1,0:T(8,128)S(1)} fusion(f32[16,64,128]{2,1,0:T(8,128)S(1)} %fusion.59, s32[256]{0:T(256)S(1)} %bitcast.183, f32[256]{0:T(256)S(1)} %get-tuple-element.127), kind=kCustom, calls=%fused_computation.1 | custom fusion | flops 256 | bytes 6144 | tf_op jit(solution)/shard_map/scatter-add | solution.py:59
  104.0 2.7 multiply_add_fusion.1
  106.7 7.2 collective-permute-start.12
  114.0 1.9 collective-permute-start.13
  115.9 0.6 dynamic-slice.25
  118.6 0.8 fusion.362
  119.4 7.2 collective-permute-start.6
  126.6 2.1 collective-permute-start.7
  128.8 8.2 fusion.34
  136.9 15.1 %scatter_fusion.2 = f32[16,64,128]{2,1,0:T(8,128)S(1)} fusion(f32[16,64,128]{2,1,0:T(8,128)S(1)} %fusion.34, s32[256]{0:T(256)S(1)} %bitcast.184, f32[256]{0:T(256)S(1)} %get-tuple-element.126), kind=kCustom, calls=%fused_computation.2 | custom fusion | flops 256 | bytes 6144 | tf_op jit(solution)/shard_map/scatter-add | solution.py:59
  152.1 10.1 %multiply_add_fusion = (f32[16,64,128]{2,1,0:T(8,128)S(1)}, f32[16,64,128]{2,1,0:T(8,128)}, f32[16,64,128]{2,1,0:T(8,128)S(1)}) fusion(f32[16,64,128]{2,1,0:T(8,128)S(1)} %copy-done, f32[16,64,128]{2,1,0:T(8,128)S(1)} %scatter-add.44, f32[16,64,128]{2,1,0:T(8,128)} %copy-done.3, f32[4,64,128]{2,1,0:T(8,128)} %collective-permute-done.7, ...), kind=kLoop, calls=%fused_computation.602 | loop fusion | flops 6553600 | bytes 3932160 | tf_op jit(solution)/shard_map/add | solution.py:86
  162.2 7.2 collective-permute-start.14
  169.5 1.9 collective-permute-start.15
  171.4 0.6 dynamic-slice.26
  174.1 0.7 fusion.361
  174.8 7.2 collective-permute-start.8
  182.1 1.9 collective-permute-start.9
  184.0 9.1 fusion.9
  193.1 15.1 %scatter_fusion.3 = f32[16,64,128]{2,1,0:T(8,128)S(1)} fusion(f32[16,64,128]{2,1,0:T(8,128)S(1)} %fusion.9, s32[256]{0:T(256)S(1)} %bitcast.185, f32[256]{0:T(256)S(1)} %get-tuple-element.43), kind=kCustom, calls=%fused_computation.3 | custom fusion | flops 256 | bytes 6144 | tf_op jit(solution)/shard_map/scatter-add | solution.py:59
  208.2 3.9 fusion.87
  212.2 1.1 fusion.357
  213.3 1.2 convolution_bitcast_fusion
  214.5 1.4 convolution_bitcast_fusion.1
  215.9 38.9 %reduce-scatter.2.cloned.1.call-done = f32[16,8,128]{2,1,0:T(8,128)} async-done(((f32[16,64,128]{2,1,0:T(8,128)}), f32[16,8,128]{2,1,0:T(8,128)}) %reduce-scatter.2.cloned.1.call-update) | async-done | bytes 65552 | tf_op jit(solution)/shard_map/reduce_scatter | solution.py:98
  254.8 0.8 broadcast_multiply_fusion
  256.5 624.8 %all-gather.1 = f32[256,12,5]{1,2,0:T(8,128)S(1)} all-gather(f32[1,12,5]{1,2,0:T(8,128)S(1)} %maximum_bitcast_fusion), channel_id=2, replica_groups=mesh['depth'=32,'shot'=8] {'depth','shot'}, dimensions={0}, use_global_device_ids=true | all-gather | bytes 61680 | tf_op jit(solution)/shard_map/all_gather | solution.py:110
  881.6 0.7 fusion.366
  882.3 0.7 fusion.367
  883.0 0.7 fusion.365
  922.4 0.7 multiply_add_fusion.2
  923.1 29.8 %all_gather.11 = f32[16,64,128]{2,1,0:T(8,128)S(1)} all-gather(f32[16,8,128]{2,1,0:T(8,128)S(1)} %get-tuple-element.41), channel_id=1, replica_groups=mesh['depth'=32,'shot'=8] {'shot'}, dimensions={1}, use_global_device_ids=true | all-gather | bytes 589824 | tf_op jit(solution)/shard_map/all_gather | solution.py:145
  952.8 0.8 copy.54
  (67 shorter events, 3.0 us)
Async XLA Ops:
  7.2 20.5 %copy-start.14 = (s32[3]{0:T(128)S(1)}, s32[3]{0:T(128)}, u32[]{:S(2)}) copy-start(s32[3]{0:T(128)} %constant.255.clone.1) | copy-start | bytes 40
  7.2 21.2 %copy-start.2 = (f32[1,16,64,128]{3,2,1,0:T(8,128)S(1)}, f32[1,16,64,128]{3,2,1,0:T(8,128)}, u32[]{:S(2)}) copy-start(f32[1,16,64,128]{3,2,1,0:T(8,128)} %param.20) | copy-start | bytes 1572868
  7.2 7.3 copy-start.1
  7.2 16.6 %copy-start.12 = (f32[1,4,256]{2,1,0:T(4,128)S(1)}, f32[1,4,256]{2,1,0:T(4,128)}, u32[]{:S(2)}) copy-start(f32[1,4,256]{2,1,0:T(4,128)} %param.24) | copy-start | bytes 12292
  7.2 16.6 %copy-start.13 = (s32[1,256]{1,0:T(1,128)S(1)}, s32[1,256]{1,0:T(1,128)}, u32[]{:S(2)}) copy-start(s32[1,256]{1,0:T(1,128)} %param.23) | copy-start | bytes 3076
  7.2 17.2 %copy-start.11 = (f32[1,4]{1,0:T(1,128)S(1)}, f32[1,4]{1,0:T(1,128)}, u32[]{:S(2)}) copy-start(f32[1,4]{1,0:T(1,128)} %param.22) | copy-start | bytes 52
  7.2 21.2 %copy-start.8 = (f32[1,16,64,128]{3,2,1,0:T(8,128)S(1)}, f32[1,16,64,128]{3,2,1,0:T(8,128)}, u32[]{:S(2)}) copy-start(f32[1,16,64,128]{3,2,1,0:T(8,128)} %param.19) | copy-start | bytes 1572868
  7.2 247.6 %reduce-scatter.2.cloned.1.call-start = ((), (), s32[]{:S(2)}) async-start(), calls=%async_computation.1 | async-start | bytes 589824 | tf_op jit(solution)/shard_map/reduce_scatter | solution.py:98
  8.7 19.7 %collective-permute-start = (f32[4,64,128]{2,1,0:T(8,128)S(1)}, f32[4,64,128]{2,1,0:T(8,128)S(1)}, u32[]{:S(2)}, u32[]{:S(2)}) collective-permute-start(f32[4,64,128]{2,1,0:T(8,128)S(1)} %get-tuple-element.70), channel_id=1, source_target_pairs={{8,0},{16,8},{24,16},{32,24},{40,32},{48,40},{56,48},{64,56},{72,6... | collective-permute-start | bytes 393224 | tf_op jit(solution)/shard_map/ppermute | solution.py:21
  12.6 15.8 %collective-permute-start.1 = (f32[4,64,128]{2,1,0:T(8,128)S(1)}, f32[4,64,128]{2,1,0:T(8,128)S(1)}, u32[]{:S(2)}, u32[]{:S(2)}) collective-permute-start(f32[4,64,128]{2,1,0:T(8,128)S(1)} %get-tuple-element.71), channel_id=1, source_target_pairs={{0,8},{8,16},{16,24},{24,32},{32,40},{40,48},{48,56},{56,64},{64,7... | collective-permute-start | bytes 393224 | tf_op jit(solution)/shard_map/ppermute | solution.py:19
  14.6 39.7 %collective-permute-start.2 = (f32[4,64,128]{2,1,0:T(8,128)S(1)}, f32[4,64,128]{2,1,0:T(8,128)S(1)}, u32[]{:S(2)}, u32[]{:S(2)}) collective-permute-start(f32[4,64,128]{2,1,0:T(8,128)S(1)} %get-tuple-element.68), channel_id=1, source_target_pairs={{8,0},{16,8},{24,16},{32,24},{40,32},{48,40},{56,48},{64,56},{72,6... | collective-permute-start | bytes 393224 | tf_op jit(solution)/shard_map/ppermute | solution.py:21
  21.8 32.4 %collective-permute-start.3 = (f32[4,64,128]{2,1,0:T(8,128)S(1)}, f32[4,64,128]{2,1,0:T(8,128)S(1)}, u32[]{:S(2)}, u32[]{:S(2)}) collective-permute-start(f32[4,64,128]{2,1,0:T(8,128)S(1)} %get-tuple-element.69), channel_id=1, source_target_pairs={{0,8},{8,16},{16,24},{24,32},{32,40},{40,48},{48,56},{56,64},{64,7... | collective-permute-start | bytes 393224 | tf_op jit(solution)/shard_map/ppermute | solution.py:19
  30.4 23.9 %copy-start = (f32[16,64,128]{2,1,0:T(8,128)S(1)}, f32[16,64,128]{2,1,0:T(8,128)}, u32[]{:S(2)}) copy-start(f32[16,64,128]{2,1,0:T(8,128)} %param.16) | copy-start | bytes 1572868
  58.0 21.8 %copy-start.5 = (f32[16,64,128]{2,1,0:T(8,128)}, f32[16,64,128]{2,1,0:T(8,128)S(1)}, u32[]{:S(2)}) copy-start(f32[16,64,128]{2,1,0:T(8,128)S(1)} %get-tuple-element.61) | copy-start | bytes 1572868
  60.7 19.0 %collective-permute-start.10 = (f32[4,64,128]{2,1,0:T(8,128)S(1)}, f32[4,64,128]{2,1,0:T(8,128)S(1)}, u32[]{:S(2)}, u32[]{:S(2)}) collective-permute-start(f32[4,64,128]{2,1,0:T(8,128)S(1)} %get-tuple-element.59), channel_id=1, source_target_pairs={{8,0},{16,8},{24,16},{32,24},{40,32},{48,40},{56,48},{64,56},{72,6... | collective-permute-start | bytes 393224 | tf_op jit(solution)/shard_map/ppermute | solution.py:21
  68.0 11.8 %collective-permute-start.11 = (f32[4,64,128]{2,1,0:T(8,128)S(1)}, f32[4,64,128]{2,1,0:T(8,128)S(1)}, u32[]{:S(2)}, u32[]{:S(2)}) collective-permute-start(f32[4,64,128]{2,1,0:T(8,128)S(1)} %get-tuple-element.60), channel_id=1, source_target_pairs={{0,8},{8,16},{16,24},{24,32},{32,40},{40,48},{48,56},{56,64},{64,7... | collective-permute-start | bytes 393224 | tf_op jit(solution)/shard_map/ppermute | solution.py:19
  70.6 33.4 %collective-permute-start.4 = (f32[4,64,128]{2,1,0:T(8,128)}, f32[4,64,128]{2,1,0:T(8,128)S(1)}, u32[]{:S(2)}, u32[]{:S(2)}) collective-permute-start(f32[4,64,128]{2,1,0:T(8,128)} %get-tuple-element.66), channel_id=1, source_target_pairs={{8,0},{16,8},{24,16},{32,24},{40,32},{48,40},{56,48},{64,56},{72,6... | collective-permute-start | bytes 393224 | tf_op jit(solution)/shard_map/ppermute | solution.py:21
  77.9 26.2 %collective-permute-start.5 = (f32[4,64,128]{2,1,0:T(8,128)S(1)}, f32[4,64,128]{2,1,0:T(8,128)S(1)}, u32[]{:S(2)}, u32[]{:S(2)}) collective-permute-start(f32[4,64,128]{2,1,0:T(8,128)S(1)} %get-tuple-element.67), channel_id=1, source_target_pairs={{0,8},{8,16},{16,24},{24,32},{32,40},{40,48},{48,56},{56,64},{64,7... | collective-permute-start | bytes 393224 | tf_op jit(solution)/shard_map/ppermute | solution.py:19
  106.7 10.5 %copy-start.6 = (f32[16,64,128]{2,1,0:T(8,128)}, f32[16,64,128]{2,1,0:T(8,128)S(1)}, u32[]{:S(2)}) copy-start(f32[16,64,128]{2,1,0:T(8,128)S(1)} %get-tuple-element.58) | copy-start | bytes 1572868
  106.7 22.0 %collective-permute-start.12 = (f32[4,64,128]{2,1,0:T(8,128)S(1)}, f32[4,64,128]{2,1,0:T(8,128)S(1)}, u32[]{:S(2)}, u32[]{:S(2)}) collective-permute-start(f32[4,64,128]{2,1,0:T(8,128)S(1)} %get-tuple-element.56), channel_id=1, source_target_pairs={{8,0},{16,8},{24,16},{32,24},{40,32},{48,40},{56,48},{64,56},{72,6... | collective-permute-start | bytes 393224 | tf_op jit(solution)/shard_map/ppermute | solution.py:21
  114.0 14.8 %collective-permute-start.13 = (f32[4,64,128]{2,1,0:T(8,128)S(1)}, f32[4,64,128]{2,1,0:T(8,128)S(1)}, u32[]{:S(2)}, u32[]{:S(2)}) collective-permute-start(f32[4,64,128]{2,1,0:T(8,128)S(1)} %get-tuple-element.57), channel_id=1, source_target_pairs={{0,8},{8,16},{16,24},{24,32},{32,40},{40,48},{48,56},{56,64},{64,7... | collective-permute-start | bytes 393224 | tf_op jit(solution)/shard_map/ppermute | solution.py:19
  118.6 18.3 %copy-start.3 = (f32[16,64,128]{2,1,0:T(8,128)}, f32[16,64,128]{2,1,0:T(8,128)S(1)}, u32[]{:S(2)}) copy-start(f32[16,64,128]{2,1,0:T(8,128)S(1)} %scatter-add.45) | copy-start | bytes 1572868
  119.4 32.7 %collective-permute-start.6 = (f32[4,64,128]{2,1,0:T(8,128)}, f32[4,64,128]{2,1,0:T(8,128)S(1)}, u32[]{:S(2)}, u32[]{:S(2)}) collective-permute-start(f32[4,64,128]{2,1,0:T(8,128)} %get-tuple-element.64), channel_id=1, source_target_pairs={{8,0},{16,8},{24,16},{32,24},{40,32},{48,40},{56,48},{64,56},{72,6... | collective-permute-start | bytes 393224 | tf_op jit(solution)/shard_map/ppermute | solution.py:21
  126.6 25.5 %collective-permute-start.7 = (f32[4,64,128]{2,1,0:T(8,128)}, f32[4,64,128]{2,1,0:T(8,128)}, u32[]{:S(2)}, u32[]{:S(2)}) collective-permute-start(f32[4,64,128]{2,1,0:T(8,128)} %get-tuple-element.65), channel_id=1, source_target_pairs={{0,8},{8,16},{16,24},{24,32},{32,40},{40,48},{48,56},{56,64},{64,7... | collective-permute-start | bytes 393224 | tf_op jit(solution)/shard_map/ppermute | solution.py:19
  162.2 10.5 %copy-start.4 = (f32[16,64,128]{2,1,0:T(8,128)}, f32[16,64,128]{2,1,0:T(8,128)S(1)}, u32[]{:S(2)}) copy-start(f32[16,64,128]{2,1,0:T(8,128)S(1)} %get-tuple-element.55) | copy-start | bytes 1572868
  162.2 21.8 %collective-permute-start.14 = (f32[4,64,128]{2,1,0:T(8,128)S(1)}, f32[4,64,128]{2,1,0:T(8,128)S(1)}, u32[]{:S(2)}, u32[]{:S(2)}) collective-permute-start(f32[4,64,128]{2,1,0:T(8,128)S(1)} %get-tuple-element.53), channel_id=1, source_target_pairs={{8,0},{16,8},{24,16},{32,24},{40,32},{48,40},{56,48},{64,56},{72,6... | collective-permute-start | bytes 393224 | tf_op jit(solution)/shard_map/ppermute | solution.py:21
  169.5 14.5 %collective-permute-start.15 = (f32[4,64,128]{2,1,0:T(8,128)S(1)}, f32[4,64,128]{2,1,0:T(8,128)}, u32[]{:S(2)}, u32[]{:S(2)}) collective-permute-start(f32[4,64,128]{2,1,0:T(8,128)S(1)} %get-tuple-element.54), channel_id=1, source_target_pairs={{0,8},{8,16},{16,24},{24,32},{32,40},{40,48},{48,56},{56,64},{64,7... | collective-permute-start | bytes 393224 | tf_op jit(solution)/shard_map/ppermute | solution.py:19
  174.8 33.4 %collective-permute-start.8 = (f32[4,64,128]{2,1,0:T(8,128)}, f32[4,64,128]{2,1,0:T(8,128)S(1)}, u32[]{:S(2)}, u32[]{:S(2)}) collective-permute-start(f32[4,64,128]{2,1,0:T(8,128)} %get-tuple-element.62), channel_id=1, source_target_pairs={{8,0},{16,8},{24,16},{32,24},{40,32},{48,40},{56,48},{64,56},{72,6... | collective-permute-start | bytes 393224 | tf_op jit(solution)/shard_map/ppermute | solution.py:21
  182.1 26.2 %collective-permute-start.9 = (f32[4,64,128]{2,1,0:T(8,128)}, f32[4,64,128]{2,1,0:T(8,128)S(1)}, u32[]{:S(2)}, u32[]{:S(2)}) collective-permute-start(f32[4,64,128]{2,1,0:T(8,128)} %get-tuple-element.63), channel_id=1, source_target_pairs={{0,8},{8,16},{16,24},{24,32},{32,40},{40,48},{48,56},{56,64},{64,7... | collective-permute-start | bytes 393224 | tf_op jit(solution)/shard_map/ppermute | solution.py:19
  255.7 625.9 %copy-start.10 = (f32[16,8,128]{2,1,0:T(8,128)}, f32[16,8,128]{2,1,0:T(8,128)S(1)}, u32[]{:S(2)}) copy-start(f32[16,8,128]{2,1,0:T(8,128)S(1)} %broadcast_multiply_fusion) | copy-start | bytes 196612
  256.5 665.9 %copy-start.7 = (f32[2,5,16,8,128]{4,3,2,1,0:T(8,128)S(1)}, f32[2,5,16,8,128]{4,3,2,1,0:T(8,128)}, u32[]{:S(2)}) copy-start(f32[2,5,16,8,128]{4,3,2,1,0:T(8,128)} %param.25) | copy-start | bytes 1966084
  256.5 665.9 %copy-start.9 = (f32[16,8,128]{2,1,0:T(8,128)S(1)}, f32[16,8,128]{2,1,0:T(8,128)}, u32[]{:S(2)}) copy-start(f32[16,8,128]{2,1,0:T(8,128)} %reduce-scatter.2.cloned.1.call-done) | copy-start | bytes 196612
Sparse Core Ops, SparseCore 0:
  212.3 42.4 reduce-scatter.1
